TPU v7x, 32 devices: a whole 2x2x4 slice. The times are simulated.
32 devices in a mesh: band: 8 (over z, core), grid: 4 (over y, x).
Axes of the slice: x: 2, y: 2, z: 4, core: 2. Of those that a mesh axis runs over, the one named last changes fastest.
Arguments:
- orbitals: float32 [8, 128, 128, 128], P('band', 'grid')
- sources: int32 [4], replicated, may hold values from 0 to 7, as said below
Outputs:
- compressed: float32 [8, 128, 128, 128], P(None, 'grid', 'band')
Inputs may be any that keep to these rules, and one draw needn't show every extreme that they name: `sources`: 4 distinct orbital indices in some order.
All inputs are finite; a program needn't handle non-finite values.
Results may differ from a plain program's by a relative error of at most 0.0003.
Values sent between devices are 32-bit elements; how exact they have to be, the bound alone decides.
A program may use at most 64 MiB of HBM per device.

v0:
```python
import math
import jax
import jax.numpy as jnp
from jax import lax
from jax.sharding import PartitionSpec as P

highest = lax.Precision.HIGHEST


def spread_2(block, axis, owner):
    block = jnp.where(lax.axis_index(axis) == owner, block, jnp.zeros_like(block))
    return lax.psum(block, axis)


def cas_table(length):
    index_values = jnp.arange(length, dtype=jnp.int32)
    products = index_values[:, None] * index_values[None, :] % length
    angles = products.astype(jnp.float32) * (2.0 * math.pi / length)
    return jnp.cos(angles) + jnp.sin(angles)


def squared_waves(start, count, length):
    index_values = start + jnp.arange(count, dtype=jnp.int32)
    signed = jnp.where(index_values < length // 2, index_values, index_values - length)
    waves = signed.astype(jnp.float32) * (2.0 * math.pi / length)
    return waves * waves


def per_device(orbitals, sources):
    band_count, slab_x, full_y, full_z = orbitals.shape
    grid_count = lax.axis_size("grid")
    full_x = slab_x * grid_count
    total_bands = band_count * lax.axis_size("band")
    round_count = sources.shape[0]
    table_x = cas_table(full_x)
    table_y = cas_table(full_y)
    table_z = cas_table(full_z)
    column_y = full_y // grid_count
    start_y = lax.axis_index("grid") * column_y
    waves = (
        squared_waves(0, full_x, full_x)[:, None, None]
        + squared_waves(start_y, column_y, full_y)[None, :, None]
        + squared_waves(0, full_z, full_z)[None, None, :]
    )
    screen = (4.0 * math.pi / full_x) ** 2
    volume = 1.0 / (full_x * full_y * full_z)
    kernel = volume / (waves + screen)

    def plane_transform(field):
        spread = jnp.einsum("bxyz,zk->bxyk", field, table_z, precision=highest)
        return jnp.einsum("bxyk,yj->bxjk", spread, table_y, precision=highest)

    def own_slab(number):
        owner = number // band_count
        local = number % band_count
        return (owner, lax.dynamic_index_in_dim(orbitals, local, 0, keepdims=False))

    def fetch(number):
        owner, slab = own_slab(number)
        return spread_2(slab, "band", owner)

    arrived = [fetch(sources[turn]) for turn in range(round_count)]
    terms = jnp.zeros(orbitals.shape, jnp.float32)
    for turn in range(round_count):
        source = arrived[turn][None]
        spectra = plane_transform(orbitals * source)
        potential_columns = lax.all_to_all(spectra, "grid", split_axis=2, concat_axis=1, tiled=True)
        line_spread = jnp.einsum("bxyz,xa->bayz", potential_columns, table_x, precision=highest)
        line_spread = line_spread * kernel[None]
        filtered = jnp.einsum("bayz,ax->bxyz", line_spread, table_x, precision=highest)
        terms = terms + source * plane_transform(
            lax.all_to_all(filtered, "grid", split_axis=1, concat_axis=2, tiled=True)
        )
    orbital_cols, term_cols = (
        lax.all_to_all(orbitals, "band", split_axis=2, concat_axis=0, tiled=True),
        lax.all_to_all(terms, "band", split_axis=2, concat_axis=0, tiled=True),
    )
    flat_orbitals = orbital_cols.reshape(total_bands, -1)
    flat_terms = term_cols.reshape(total_bands, -1)
    partial_intersection = (
        jnp.dot(flat_orbitals, flat_terms.T, precision=highest, preferred_element_type=jnp.float32)
        * volume
    )
    intersection = lax.psum(partial_intersection, ("band", "grid"))
    factor = jnp.linalg.cholesky(intersection)
    solved = lax.linalg.triangular_solve(factor, flat_terms, left_side=True, lower=True)
    return (-solved).reshape(term_cols.shape)


def solution(mesh):
    placed = (P("band", "grid", None, None), P())
    return jax.shard_map(
        per_device,
        mesh=mesh,
        in_specs=placed,
        out_specs=P(None, "grid", "band", None),
        check_vma=False,
    )
```

profile of v0, /device:TPU:10, one launch (start us, length us, event | category | flops | bytes accessed | tf_op | source)
XLA Modules:
  0.0 616.8 jit_solution(3678246858079370884)
XLA Ops:
  10.5 5.3 broadcast_select_fusion.3
  15.9 176.9 %all-reduce.3.cloned.1.call-done = (f32[1,32,128,128]{3,2,1,0:T(8,128)}, f32[1,32,128,128]{3,2,1,0:T(8,128)}, f32[1,32,128,128]{3,2,1,0:T(8,128)}, f32[1,32,128,128]{3,2,1,0:T(8,128)}) async-done(((f32[1,32,128,128]{3,2,1,0:T(8,128)}, f32[1,32,128,128]{3,2,1,0:T(8,128)}, f32[1,32,128,128]{3,2,1,0:T(8,128)}, f32[1,32,128,128]{3,2,1,0:T(8,128)}), (f32[1,32,128,128]{3,2,1,0:T(8,128)}, ...) | async-done | bytes 8388624 | tf_op jit(solution)/shard_map/psum | solution.py:12
  192.8 3.7 fusion.11
  196.5 2.2 convolution_bitcast_fusion.2
  198.7 2.5 copy.56
  201.2 5.2 all-to-all-start.2
  206.4 3.7 fusion.13
  210.1 2.2 convolution_bitcast_fusion.3
  212.3 2.6 copy.48
  214.9 15.8 %all-to-all-done.2 = f32[1,32,128,128]{3,1,0,2:T(8,128)} async-done(((f32[1,32,128,128]{3,1,0,2:T(8,128)}), f32[1,32,128,128]{3,1,0,2:T(8,128)}, u32[]{:S(2)}, u32[]{:S(2)}) %all-to-all-start.2) | async-done | bytes 2097184 | tf_op jit(solution)/shard_map/all_to_all | solution.py:67
  230.7 5.0 all-to-all-start
  235.7 3.7 fusion.9
  239.4 2.2 convolution_bitcast_fusion.1
  241.6 2.5 copy.64
  244.2 15.5 %all-to-all-done = f32[1,32,128,128]{3,1,0,2:T(8,128)} async-done(((f32[1,32,128,128]{3,1,0,2:T(8,128)}), f32[1,32,128,128]{3,1,0,2:T(8,128)}, u32[]{:S(2)}, u32[]{:S(2)}) %all-to-all-start) | async-done | bytes 2097184 | tf_op jit(solution)/shard_map/all_to_all | solution.py:67
  259.7 5.5 all-to-all-start.4
  265.2 3.7 fusion.7
  268.9 2.2 convolution_bitcast_fusion
  271.1 2.5 copy.72
  273.6 15.5 %all-to-all-done.4 = f32[1,32,128,128]{3,1,0,2:T(8,128)} async-done(((f32[1,32,128,128]{3,1,0,2:T(8,128)}), f32[1,32,128,128]{3,1,0,2:T(8,128)}, u32[]{:S(2)}, u32[]{:S(2)}) %all-to-all-start.4) | async-done | bytes 2097184 | tf_op jit(solution)/shard_map/all_to_all | solution.py:67
  289.0 5.0 all-to-all-start.6
  294.2 2.8 copy.57
  297.2 3.2 fusion.19
  300.4 2.5 fusion.38
  302.9 2.5 copy.60
  305.4 12.6 %all-to-all-done.6 = f32[1,32,128,128]{3,1,0,2:T(8,128)} async-done(((f32[1,32,128,128]{3,1,0,2:T(8,128)}), f32[1,32,128,128]{3,1,0,2:T(8,128)}, u32[]{:S(2)}, u32[]{:S(2)}) %all-to-all-start.6) | async-done | bytes 2097184 | tf_op jit(solution)/shard_map/all_to_all | solution.py:67
  318.0 5.2 all-to-all-start.3
  323.2 2.8 copy.49
  326.3 3.2 fusion.21
  329.5 2.5 fusion.35
  331.9 2.5 copy.52
  334.5 12.6 %all-to-all-done.3 = f32[1,128,32,128]{3,2,0,1:T(8,128)} async-done(((f32[1,128,32,128]{3,2,0,1:T(8,128)}), f32[1,128,32,128]{3,2,0,1:T(8,128)}, u32[]{:S(2)}, u32[]{:S(2)}) %all-to-all-start.3) | async-done | bytes 2097184 | tf_op jit(solution)/shard_map/all_to_all | solution.py:72
  347.1 5.2 all-to-all-start.1
  352.3 2.8 copy.65
  355.4 3.2 fusion.17
  358.5 2.5 fusion.41
  361.0 2.5 copy.68
  363.6 12.7 %all-to-all-done.1 = f32[1,128,32,128]{3,2,0,1:T(8,128)} async-done(((f32[1,128,32,128]{3,2,0,1:T(8,128)}), f32[1,128,32,128]{3,2,0,1:T(8,128)}, u32[]{:S(2)}, u32[]{:S(2)}) %all-to-all-start.1) | async-done | bytes 2097184 | tf_op jit(solution)/shard_map/all_to_all | solution.py:72
  376.3 5.5 all-to-all-start.5
  381.7 2.8 copy.73
  384.8 3.2 fusion.15
  387.9 2.5 fusion.44
  390.4 2.6 copy.76
  394.8 3.2 copy.53
  398.0 3.4 fusion.71
  401.4 4.3 all-to-all-done.5
  405.7 5.1 all-to-all-start.7
  413.0 3.5 fusion.86
  416.5 2.2 fusion.74
  418.7 3.5 fusion.91
  422.2 2.2 fusion.68
  424.3 3.5 fusion.81
  427.8 6.8 %all-to-all-done.7 = f32[1,128,32,128]{3,2,0,1:T(8,128)} async-done(((f32[1,128,32,128]{3,2,0,1:T(8,128)}), f32[1,128,32,128]{3,2,0,1:T(8,128)}, u32[]{:S(2)}, u32[]{:S(2)}) %all-to-all-start.7) | async-done | bytes 2097184 | tf_op jit(solution)/shard_map/all_to_all | solution.py:72
  436.6 2.4 fusion.65
  439.0 6.3 %fusion.3 = f32[1,32,128,128]{3,2,1,0:T(8,128)S(1)} fusion(f32[1,32,128,128]{3,2,1,0:T(8,128)S(1)} %copy-done.1, f32[1,32,128,128]{3,2,1,0:T(8,128)S(1)} %copy-done.2, f32[128,32,128]{2,0,1:T(8,128)} %fusion.81, f32[1,32,128,128]{3,2,1,0:T(8,128)S(1)} %copy-done.3, f32[128,32,128]{2,0,1:T(8,128)} %fusion.86, f32[1,32,128,128]{3,2,1,0:T(8,128)S(1)} %copy-done.4, ...), kind=kOutput, calls=%fused_computation.5 | convolution fusion | flops 809222144 | bytes 18874368 | tf_op jit(solution)/shard_map/bxyk,yj->bxjk/dot_general | solution.py:51
  445.3 2.5 copy.79
  447.8 4.8 all-to-all-start.8
  452.6 2.6 copy.82
  455.1 43.0 %all-to-all-done.8 = f32[1,32,128,128]{3,1,0,2:T(8,128)} async-done(((f32[1,32,128,128]{3,1,0,2:T(8,128)}), f32[1,32,128,128]{3,1,0,2:T(8,128)}, u32[]{:S(2)}, u32[]{:S(2)}) %all-to-all-start.8) | async-done | bytes 2097184 | tf_op jit(solution)/shard_map/all_to_all | solution.py:76
  498.2 8.1 %all-to-all-start.9 = ((f32[1,32,128,128]{3,1,0,2:T(8,128)}), f32[1,32,128,128]{3,1,0,2:T(8,128)}, u32[]{:S(2)}, u32[]{:S(2)}) async-start(f32[1,32,128,128]{3,1,0,2:T(8,128)} %copy.82), calls=%async_computation.9 | async-start | bytes 4194304 | tf_op jit(solution)/shard_map/all_to_all | solution.py:75
  506.3 2.8 copy.81
  509.1 42.7 %all-to-all-done.9 = f32[1,32,128,128]{3,1,0,2:T(8,128)} async-done(((f32[1,32,128,128]{3,1,0,2:T(8,128)}), f32[1,32,128,128]{3,1,0,2:T(8,128)}, u32[]{:S(2)}, u32[]{:S(2)}) %all-to-all-start.9) | async-done | bytes 2097184 | tf_op jit(solution)/shard_map/all_to_all | solution.py:75
  551.8 9.3 %fusion.57 = f32[8,8]{0,1:T(8,128)S(1)} fusion(f32[1,32,8,16,128]{4,1,3,2,0:T(8,128)} %bitcast.64, f32[1,32,8,16,128]{4,1,3,2,0:T(8,128)} %bitcast.61), kind=kOutput, calls=%fused_computation.51 | convolution fusion | flops 50331712 | bytes 4194560 | tf_op jit(solution)/shard_map/dot_general | solution.py:81
  561.1 42.1 %psum.39 = f32[8,8]{0,1:T(8,128)S(1)} all-reduce(f32[8,8]{0,1:T(8,128)S(1)} %fusion.57), channel_id=1, replica_groups=mesh['band'=8,'grid'=4] {'band','grid'}, use_global_device_ids=true, to_apply=%region_4.5 | all-reduce | flops 64 | bytes 512 | tf_op jit(solution)/shard_map/psum | solution.py:84
  (36 shorter events, 14.8 us)
Async XLA Ops:
  6.5 186.2 %all-reduce.3.cloned.1.call-start = ((), (), s32[]{:S(2)}) async-start(), calls=%async_computation.10 | async-start | bytes 16777216 | tf_op jit(solution)/shard_map/psum | solution.py:12
  15.9 176.9 %copy-start = (f32[1,32,128,128]{3,2,1,0:T(8,128)S(1)}, f32[1,32,128,128]{3,2,1,0:T(8,128)}, u32[]{:S(2)}) copy-start(f32[1,32,128,128]{3,2,1,0:T(8,128)} %param.2) | copy-start | bytes 6291460
  201.2 29.5 %all-to-all-start.2 = ((f32[1,32,128,128]{3,1,0,2:T(8,128)}), f32[1,32,128,128]{3,1,0,2:T(8,128)}, u32[]{:S(2)}, u32[]{:S(2)}) async-start(f32[1,32,128,128]{3,1,0,2:T(8,128)} %copy.56), calls=%async_computation.2 | async-start | bytes 4194304 | tf_op jit(solution)/shard_map/all_to_all | solution.py:67
  230.7 28.9 %all-to-all-start = ((f32[1,32,128,128]{3,1,0,2:T(8,128)}), f32[1,32,128,128]{3,1,0,2:T(8,128)}, u32[]{:S(2)}, u32[]{:S(2)}) async-start(f32[1,32,128,128]{3,1,0,2:T(8,128)} %copy.48), calls=%async_computation | async-start | bytes 4194304 | tf_op jit(solution)/shard_map/all_to_all | solution.py:67
  259.7 29.4 %all-to-all-start.4 = ((f32[1,32,128,128]{3,1,0,2:T(8,128)}), f32[1,32,128,128]{3,1,0,2:T(8,128)}, u32[]{:S(2)}, u32[]{:S(2)}) async-start(f32[1,32,128,128]{3,1,0,2:T(8,128)} %copy.64), calls=%async_computation.4 | async-start | bytes 4194304 | tf_op jit(solution)/shard_map/all_to_all | solution.py:67
  289.0 29.0 %all-to-all-start.6 = ((f32[1,32,128,128]{3,1,0,2:T(8,128)}), f32[1,32,128,128]{3,1,0,2:T(8,128)}, u32[]{:S(2)}, u32[]{:S(2)}) async-start(f32[1,32,128,128]{3,1,0,2:T(8,128)} %copy.72), calls=%async_computation.6 | async-start | bytes 4194304 | tf_op jit(solution)/shard_map/all_to_all | solution.py:67
  318.0 29.1 %all-to-all-start.3 = ((f32[1,128,32,128]{3,2,0,1:T(8,128)}), f32[1,128,32,128]{3,2,0,1:T(8,128)}, u32[]{:S(2)}, u32[]{:S(2)}) async-start(f32[1,128,32,128]{3,2,0,1:T(8,128)} %copy.60), calls=%async_computation.3 | async-start | bytes 4194304 | tf_op jit(solution)/shard_map/all_to_all | solution.py:72
  347.1 29.1 %all-to-all-start.1 = ((f32[1,128,32,128]{3,2,0,1:T(8,128)}), f32[1,128,32,128]{3,2,0,1:T(8,128)}, u32[]{:S(2)}, u32[]{:S(2)}) async-start(f32[1,128,32,128]{3,2,0,1:T(8,128)} %copy.52), calls=%async_computation.1 | async-start | bytes 4194304 | tf_op jit(solution)/shard_map/all_to_all | solution.py:72
  376.3 29.4 %all-to-all-start.5 = ((f32[1,128,32,128]{3,2,0,1:T(8,128)}), f32[1,128,32,128]{3,2,0,1:T(8,128)}, u32[]{:S(2)}, u32[]{:S(2)}) async-start(f32[1,128,32,128]{3,2,0,1:T(8,128)} %copy.68), calls=%async_computation.5 | async-start | bytes 4194304 | tf_op jit(solution)/shard_map/all_to_all | solution.py:72
  405.7 28.9 %all-to-all-start.7 = ((f32[1,128,32,128]{3,2,0,1:T(8,128)}), f32[1,128,32,128]{3,2,0,1:T(8,128)}, u32[]{:S(2)}, u32[]{:S(2)}) async-start(f32[1,128,32,128]{3,2,0,1:T(8,128)} %copy.76), calls=%async_computation.7 | async-start | bytes 4194304 | tf_op jit(solution)/shard_map/all_to_all | solution.py:72
  410.8 2.2 copy-start.6
  413.0 3.5 copy-start.5
  434.6 4.4 copy-start.3
  434.6 4.4 copy-start.4
  436.6 2.4 copy-start.1
  436.6 2.4 copy-start.2
  447.8 50.4 %all-to-all-start.8 = ((f32[1,32,128,128]{3,1,0,2:T(8,128)}), f32[1,32,128,128]{3,1,0,2:T(8,128)}, u32[]{:S(2)}, u32[]{:S(2)}) async-start(f32[1,32,128,128]{3,1,0,2:T(8,128)} %copy.79), calls=%async_computation.8 | async-start | bytes 4194304 | tf_op jit(solution)/shard_map/all_to_all | solution.py:76
  498.2 53.6 %all-to-all-start.9 = ((f32[1,32,128,128]{3,1,0,2:T(8,128)}), f32[1,32,128,128]{3,1,0,2:T(8,128)}, u32[]{:S(2)}, u32[]{:S(2)}) async-start(f32[1,32,128,128]{3,1,0,2:T(8,128)} %copy.82), calls=%async_computation.9 | async-start | bytes 4194304 | tf_op jit(solution)/shard_map/all_to_all | solution.py:75
Sparse Core Ops, SparseCore 0:
  16.0 176.7 all-reduce.2
where the time goes:
time: 623 us; the launch traced here: 617 us
  waiting for transfers between devices  358 us (57%)
  matrix products  84 us (13%)
  starting transfers between devices  54.6 us (9%)
  local copies, waits for them, and re-layouts  52.8 us (8%)
  blocking collectives  42.1 us (7%)
  between operations  16.7 us (3%)
  other arithmetic  8.11 us (1%)
    psum x1, waiting for transfers between devices, spread_2(): return lax.psum(block, axis)  177 us
    all_to_all x4, waiting for transfers between devices, per_device(): lax.all_to_all(spectra, 'grid', split_axis=2, concat_axis=1, tiled=True)  59.4 us
    all_to_all x1, waiting for transfers between devices, per_device(): lax.all_to_all(terms, 'band', split_axis=2, concat_axis=0, tiled=True)  43 us
    all_to_all x1, waiting for transfers between devices, per_device(): lax.all_to_all(orbitals, 'band', split_axis=2, concat_axis=0, tiled=True)  42.7 us
    psum x1, blocking collectives, per_device(): intersection = lax.psum(partial_intersection, ('band', 'grid'))  42.1 us
    all_to_all x4, waiting for transfers between devices, per_device(): lax.all_to_all(filtered, 'grid', split_axis=1, concat_axis=2, tiled=True)  36.4 us
    dot_general x8, matrix products, plane_transform(): return jnp.einsum('bxyk,yj->bxjk', spread, table_y, precision=highest)  25.4 us
    dot_general x8, matrix products, plane_transform(): spread = jnp.einsum('bxyz,zk->bxyk', field, table_z, precision=highest)  24.9 us
  transfers between devices with their start and end apart: 11, of which 11 were waited for; matrix products, arithmetic and copies ran while one was open for 16% of the time, Pallas kernels for 0%

commit v1 on v0

--- a/solution.py
+++ b/solution.py
@@ -5,6 +5,29 @@
 from jax.sharding import PartitionSpec as P
 
 highest = lax.Precision.HIGHEST
+
+
+def cut_along(shard, dim, count):
+    lengths = shard.shape
+    pieces = shard.reshape(*lengths[:dim], count, lengths[dim] // count, *lengths[dim + 1 :])
+    return jnp.moveaxis(pieces, dim, 0)
+
+
+def joined_along(parts, dim):
+    shape = list(parts.shape[1:])
+    shape[dim] *= parts.shape[0]
+    return jnp.moveaxis(parts, 0, dim).reshape(shape)
+
+
+def exchange_in_pairs(x, axis, split_dim, concat_dim):
+    size, here = (lax.axis_size(axis), lax.axis_index(axis))
+    blocks = cut_along(x, split_dim, size)
+    finished = [blocks[here]]
+    for step in range(1, size):
+        sent = blocks[here ^ step]
+        finished.append(lax.ppermute(sent, axis, [(i, i ^ step) for i in range(size)]))
+    blocks = jnp.stack(finished)[here ^ jnp.arange(size)]
+    return joined_along(blocks, concat_dim)
 
 
 def spread_2(block, axis, owner):
@@ -73,7 +96,7 @@
         )
     orbital_cols, term_cols = (
         lax.all_to_all(orbitals, "band", split_axis=2, concat_axis=0, tiled=True),
-        lax.all_to_all(terms, "band", split_axis=2, concat_axis=0, tiled=True),
+        exchange_in_pairs(terms, "band", 2, 0),
     )
     flat_orbitals = orbital_cols.reshape(total_bands, -1)
     flat_terms = term_cols.reshape(total_bands, -1)

time: 623 us -> 604 us (0.970)
  waiting for transfers between devices: 358 us -> 350 us
    ppermute x0 -> x7, waiting for transfers between devices: none -> 71 us  [exchange_in_pairs(): lax.ppermute(sent, axis, [(i, i ^ step) for i in range(size)])]
    all_to_all x1 -> x0, waiting for transfers between devices: 43 us -> none  [per_device(): lax.all_to_all(terms, 'band', split_axis=2, concat_axis=0, tiled=True)]
    all_to_all x1, waiting for transfers between devices: 42.7 us -> 0.01 us  [per_device(): lax.all_to_all(orbitals, 'band', split_axis=2, concat_axis=0, tiled=True)]
    ppermute x0 -> x7, starting transfers between devices: none -> 7.61 us  [exchange_in_pairs(): lax.ppermute(sent, axis, [(i, i ^ step) for i in range(size)])]
    all_to_all x4, waiting for transfers between devices: 36.4 us -> 42.6 us  [per_device(): lax.all_to_all(filtered, 'grid', split_axis=1, concat_axis=2, tiled=True)]
  transfers between devices with their start and end apart: 11 -> 17, of which waited for: 11 -> 15; matrix products, arithmetic and copies ran while one was open for 16% -> 18% of each run, Pallas kernels for 0% -> 0%
where the time goes in v1:
time: 604 us; the launch traced here: 596 us
  waiting for transfers between devices  350 us (58%)
  matrix products  77.8 us (13%)
  starting transfers between devices  54.3 us (9%)
  local copies, waits for them, and re-layouts  50.5 us (8%)
  blocking collectives  38.4 us (6%)
  between operations  16.7 us (3%)
  other arithmetic  8.09 us (1%)
    psum x1, waiting for transfers between devices, spread_2(): return lax.psum(block, axis)  177 us
    ppermute x7, waiting for transfers between devices, exchange_in_pairs(): lax.ppermute(sent, axis, [(i, i ^ step) for i in range(size)])  71 us
    all_to_all x4, waiting for transfers between devices, per_device(): lax.all_to_all(spectra, 'grid', split_axis=2, concat_axis=1, tiled=True)  59.4 us
    all_to_all x4, waiting for transfers between devices, per_device(): lax.all_to_all(filtered, 'grid', split_axis=1, concat_axis=2, tiled=True)  42.6 us
    psum x1, blocking collectives, per_device(): intersection = lax.psum(partial_intersection, ('band', 'grid'))  38.4 us
    dot_general x8, matrix products, plane_transform(): spread = jnp.einsum('bxyz,zk->bxyk', field, table_z, precision=highest)  23.4 us
    all_to_all x4, starting transfers between devices, per_device(): lax.all_to_all(filtered, 'grid', split_axis=1, concat_axis=2, tiled=True)  21.3 us
    dot_general x8, matrix products, plane_transform(): return jnp.einsum('bxyk,yj->bxjk', spread, table_y, precision=highest)  21.2 us
  transfers between devices with their start and end apart: 17, of which 15 were waited for; matrix products, arithmetic and copies ran while one was open for 18% of the time, Pallas kernels for 0%

profile of v1, /device:TPU:10, one launch (start us, length us, event | category | flops | bytes accessed | tf_op | source)
XLA Modules:
  0.0 595.8 jit_solution(10612311255756654816)
XLA Ops:
  10.6 5.3 broadcast_select_fusion.3
  15.9 176.9 %all-reduce.3.cloned.1.call-done = (f32[1,32,128,128]{3,2,1,0:T(8,128)}, f32[1,32,128,128]{3,2,1,0:T(8,128)}, f32[1,32,128,128]{3,2,1,0:T(8,128)}, f32[1,32,128,128]{3,2,1,0:T(8,128)}) async-done(((f32[1,32,128,128]{3,2,1,0:T(8,128)}, f32[1,32,128,128]{3,2,1,0:T(8,128)}, f32[1,32,128,128]{3,2,1,0:T(8,128)}, f32[1,32,128,128]{3,2,1,0:T(8,128)}), (f32[1,32,128,128]{3,2,1,0:T(8,128)}, ...) | async-done | bytes 8388624 | tf_op jit(solution)/shard_map/psum | solution.py:35
  192.8 3.7 fusion.12
  196.5 2.2 convolution_bitcast_fusion.2
  198.7 2.5 copy.55
  201.3 5.2 all-to-all-start.2
  206.4 3.7 fusion.14
  210.1 2.2 convolution_bitcast_fusion.3
  212.3 2.6 copy.47
  214.9 15.9 %all-to-all-done.2 = f32[1,32,128,128]{3,1,0,2:T(8,128)} async-done(((f32[1,32,128,128]{3,1,0,2:T(8,128)}), f32[1,32,128,128]{3,1,0,2:T(8,128)}, u32[]{:S(2)}, u32[]{:S(2)}) %all-to-all-start.2) | async-done | bytes 2097184 | tf_op jit(solution)/shard_map/all_to_all | solution.py:90
  230.8 5.0 all-to-all-start
  235.8 3.7 fusion.10
  239.5 2.2 convolution_bitcast_fusion.1
  241.7 2.5 copy.63
  244.2 15.5 %all-to-all-done = f32[1,32,128,128]{3,1,0,2:T(8,128)} async-done(((f32[1,32,128,128]{3,1,0,2:T(8,128)}), f32[1,32,128,128]{3,1,0,2:T(8,128)}, u32[]{:S(2)}, u32[]{:S(2)}) %all-to-all-start) | async-done | bytes 2097184 | tf_op jit(solution)/shard_map/all_to_all | solution.py:90
  259.7 5.2 all-to-all-start.4
  265.0 3.7 fusion.8
  268.7 2.2 convolution_bitcast_fusion
  270.9 2.6 copy.71
  273.4 15.4 %all-to-all-done.4 = f32[1,32,128,128]{3,1,0,2:T(8,128)} async-done(((f32[1,32,128,128]{3,1,0,2:T(8,128)}), f32[1,32,128,128]{3,1,0,2:T(8,128)}, u32[]{:S(2)}, u32[]{:S(2)}) %all-to-all-start.4) | async-done | bytes 2097184 | tf_op jit(solution)/shard_map/all_to_all | solution.py:90
  288.9 5.1 all-to-all-start.6
  294.0 2.8 copy.56
  297.1 3.2 fusion.21
  300.2 2.5 fusion.40
  302.7 2.5 copy.59
  305.2 12.6 %all-to-all-done.6 = f32[1,32,128,128]{3,1,0,2:T(8,128)} async-done(((f32[1,32,128,128]{3,1,0,2:T(8,128)}), f32[1,32,128,128]{3,1,0,2:T(8,128)}, u32[]{:S(2)}, u32[]{:S(2)}) %all-to-all-start.6) | async-done | bytes 2097184 | tf_op jit(solution)/shard_map/all_to_all | solution.py:90
  317.9 5.4 all-to-all-start.3
  323.3 2.8 copy.48
  326.4 3.2 fusion.23
  329.5 2.5 fusion.37
  332.0 2.6 copy.51
  334.6 12.6 %all-to-all-done.3 = f32[1,128,32,128]{3,2,0,1:T(8,128)} async-done(((f32[1,128,32,128]{3,2,0,1:T(8,128)}), f32[1,128,32,128]{3,2,0,1:T(8,128)}, u32[]{:S(2)}, u32[]{:S(2)}) %all-to-all-start.3) | async-done | bytes 2097184 | tf_op jit(solution)/shard_map/all_to_all | solution.py:95
  347.2 5.2 all-to-all-start.1
  352.4 2.8 copy.64
  355.5 3.2 fusion.19
  358.6 2.5 fusion.43
  361.1 2.5 copy.67
  363.7 12.7 %all-to-all-done.1 = f32[1,128,32,128]{3,2,0,1:T(8,128)} async-done(((f32[1,128,32,128]{3,2,0,1:T(8,128)}), f32[1,128,32,128]{3,2,0,1:T(8,128)}, u32[]{:S(2)}, u32[]{:S(2)}) %all-to-all-start.1) | async-done | bytes 2097184 | tf_op jit(solution)/shard_map/all_to_all | solution.py:95
  376.4 5.2 all-to-all-start.5
  381.6 2.8 copy.72
  384.6 3.2 fusion.17
  387.8 2.5 fusion.46
  390.3 2.5 copy.75
  392.8 12.7 %all-to-all-done.5 = f32[1,128,32,128]{3,2,0,1:T(8,128)} async-done(((f32[1,128,32,128]{3,2,0,1:T(8,128)}), f32[1,128,32,128]{3,2,0,1:T(8,128)}, u32[]{:S(2)}, u32[]{:S(2)}) %all-to-all-start.5) | async-done | bytes 2097184 | tf_op jit(solution)/shard_map/all_to_all | solution.py:95
  405.5 5.4 all-to-all-start.7
  411.0 2.6 copy.78
  421.2 3.5 fusion.88
  426.8 3.5 fusion.93
  430.3 4.6 all-to-all-done.7
  434.9 4.9 all-to-all-start.8
  444.0 2.2 fusion.83
  446.2 2.2 fusion.67
  448.4 3.4 fusion.4
  454.8 2.4 collective-permute-start.3
  459.0 21.9 %collective-permute-done.1 = f32[1,32,16,128]{3,2,1,0:T(8,128)S(1)} collective-permute-done((f32[1,32,16,128]{3,2,1,0:T(8,128)}, f32[1,32,16,128]{3,2,1,0:T(8,128)S(1)}, u32[]{:S(2)}, u32[]{:S(2)}) %collective-permute-start.1) | collective-permute-done | bytes 262176 | tf_op jit(solution)/shard_map/ppermute | solution.py:28
  482.4 3.6 collective-permute-done.2
  486.0 27.3 %collective-permute-done.3 = f32[1,32,16,128]{3,2,1,0:T(8,128)S(1)} collective-permute-done((f32[1,32,16,128]{3,2,1,0:T(8,128)S(1)}, f32[1,32,16,128]{3,2,1,0:T(8,128)S(1)}, u32[]{:S(2)}, u32[]{:S(2)}) %collective-permute-start.3) | collective-permute-done | bytes 262176 | tf_op jit(solution)/shard_map/ppermute | solution.py:28
  513.3 5.6 collective-permute-done.4
  518.9 8.2 %collective-permute-done.5 = f32[1,32,16,128]{3,2,1,0:T(8,128)S(1)} collective-permute-done((f32[1,32,16,128]{3,2,1,0:T(8,128)S(1)}, f32[1,32,16,128]{3,2,1,0:T(8,128)S(1)}, u32[]{:S(2)}, u32[]{:S(2)}) %collective-permute-start.5) | collective-permute-done | bytes 262176 | tf_op jit(solution)/shard_map/ppermute | solution.py:28
  527.1 4.5 collective-permute-done.6
  532.9 2.3 gather_fusion
  535.2 7.7 %fusion.59 = f32[8,8]{0,1:T(8,128)S(1)} fusion(f32[1,32,8,16,128]{4,1,3,2,0:T(8,128)} %bitcast.79, f32[8,32,16,128]{3,2,1,0:T(8,128)S(1)} %gather_fusion), kind=kOutput, calls=%fused_computation.54 | convolution fusion | flops 50331712 | bytes 4194560 | tf_op jit(solution)/shard_map/dot_general | solution.py:104
  542.9 38.4 %psum.39 = f32[8,8]{0,1:T(8,128)S(1)} all-reduce(f32[8,8]{0,1:T(8,128)S(1)} %fusion.59), channel_id=1, replica_groups=mesh['band'=8,'grid'=4] {'band','grid'}, use_global_device_ids=true, to_apply=%region_4.5 | all-reduce | flops 64 | bytes 512 | tf_op jit(solution)/shard_map/psum | solution.py:107
  584.1 2.9 convolution_negate_fusion
  (60 shorter events, 28.5 us)
Async XLA Ops:
  6.5 186.3 %all-reduce.3.cloned.1.call-start = ((), (), s32[]{:S(2)}) async-start(), calls=%async_computation.9 | async-start | bytes 16777216 | tf_op jit(solution)/shard_map/psum | solution.py:35
  15.9 176.9 %copy-start = (f32[1,32,128,128]{3,2,1,0:T(8,128)S(1)}, f32[1,32,128,128]{3,2,1,0:T(8,128)}, u32[]{:S(2)}) copy-start(f32[1,32,128,128]{3,2,1,0:T(8,128)} %param.2) | copy-start | bytes 6291460
  201.3 29.5 %all-to-all-start.2 = ((f32[1,32,128,128]{3,1,0,2:T(8,128)}), f32[1,32,128,128]{3,1,0,2:T(8,128)}, u32[]{:S(2)}, u32[]{:S(2)}) async-start(f32[1,32,128,128]{3,1,0,2:T(8,128)} %copy.55), calls=%async_computation.2 | async-start | bytes 4194304 | tf_op jit(solution)/shard_map/all_to_all | solution.py:90
  230.8 29.0 %all-to-all-start = ((f32[1,32,128,128]{3,1,0,2:T(8,128)}), f32[1,32,128,128]{3,1,0,2:T(8,128)}, u32[]{:S(2)}, u32[]{:S(2)}) async-start(f32[1,32,128,128]{3,1,0,2:T(8,128)} %copy.47), calls=%async_computation | async-start | bytes 4194304 | tf_op jit(solution)/shard_map/all_to_all | solution.py:90
  259.7 29.1 %all-to-all-start.4 = ((f32[1,32,128,128]{3,1,0,2:T(8,128)}), f32[1,32,128,128]{3,1,0,2:T(8,128)}, u32[]{:S(2)}, u32[]{:S(2)}) async-start(f32[1,32,128,128]{3,1,0,2:T(8,128)} %copy.63), calls=%async_computation.4 | async-start | bytes 4194304 | tf_op jit(solution)/shard_map/all_to_all | solution.py:90
  288.9 29.0 %all-to-all-start.6 = ((f32[1,32,128,128]{3,1,0,2:T(8,128)}), f32[1,32,128,128]{3,1,0,2:T(8,128)}, u32[]{:S(2)}, u32[]{:S(2)}) async-start(f32[1,32,128,128]{3,1,0,2:T(8,128)} %copy.71), calls=%async_computation.6 | async-start | bytes 4194304 | tf_op jit(solution)/shard_map/all_to_all | solution.py:90
  317.9 29.3 %all-to-all-start.3 = ((f32[1,128,32,128]{3,2,0,1:T(8,128)}), f32[1,128,32,128]{3,2,0,1:T(8,128)}, u32[]{:S(2)}, u32[]{:S(2)}) async-start(f32[1,128,32,128]{3,2,0,1:T(8,128)} %copy.59), calls=%async_computation.3 | async-start | bytes 4194304 | tf_op jit(solution)/shard_map/all_to_all | solution.py:95
  347.2 29.2 %all-to-all-start.1 = ((f32[1,128,32,128]{3,2,0,1:T(8,128)}), f32[1,128,32,128]{3,2,0,1:T(8,128)}, u32[]{:S(2)}, u32[]{:S(2)}) async-start(f32[1,128,32,128]{3,2,0,1:T(8,128)} %copy.51), calls=%async_computation.1 | async-start | bytes 4194304 | tf_op jit(solution)/shard_map/all_to_all | solution.py:95
  376.4 29.2 %all-to-all-start.5 = ((f32[1,128,32,128]{3,2,0,1:T(8,128)}), f32[1,128,32,128]{3,2,0,1:T(8,128)}, u32[]{:S(2)}, u32[]{:S(2)}) async-start(f32[1,128,32,128]{3,2,0,1:T(8,128)} %copy.67), calls=%async_computation.5 | async-start | bytes 4194304 | tf_op jit(solution)/shard_map/all_to_all | solution.py:95
  405.5 29.3 %all-to-all-start.7 = ((f32[1,128,32,128]{3,2,0,1:T(8,128)}), f32[1,128,32,128]{3,2,0,1:T(8,128)}, u32[]{:S(2)}, u32[]{:S(2)}) async-start(f32[1,128,32,128]{3,2,0,1:T(8,128)} %copy.75), calls=%async_computation.7 | async-start | bytes 4194304 | tf_op jit(solution)/shard_map/all_to_all | solution.py:95
  434.9 100.4 %all-to-all-start.8 = ((f32[1,32,128,128]{3,1,0,2:T(8,128)}), f32[1,32,128,128]{3,1,0,2:T(8,128)}, u32[]{:S(2)}, u32[]{:S(2)}) async-start(f32[1,32,128,128]{3,1,0,2:T(8,128)} %copy.78), calls=%async_computation.8 | async-start | bytes 4194304 | tf_op jit(solution)/shard_map/all_to_all | solution.py:98
  442.0 6.4 %copy-start.5 = (f32[128,32,128]{2,0,1:T(8,128)S(1)}, f32[128,32,128]{2,0,1:T(8,128)}, u32[]{:S(2)}) copy-start(f32[128,32,128]{2,0,1:T(8,128)} %fusion.88) | copy-start | bytes 6291460
  442.0 6.4 %copy-start.6 = (f32[128,32,128]{2,0,1:T(8,128)S(1)}, f32[128,32,128]{2,0,1:T(8,128)}, u32[]{:S(2)}) copy-start(f32[128,32,128]{2,0,1:T(8,128)} %fusion.93) | copy-start | bytes 6291460
  443.9 4.4 copy-start.3
  443.9 4.4 copy-start.4
  446.1 2.2 copy-start.1
  446.2 2.3 copy-start.2
  452.8 4.7 collective-permute-start
  452.9 27.9 %collective-permute-start.1 = (f32[1,32,16,128]{3,2,1,0:T(8,128)}, f32[1,32,16,128]{3,2,1,0:T(8,128)S(1)}, u32[]{:S(2)}, u32[]{:S(2)}) collective-permute-start(f32[1,32,16,128]{3,2,1,0:T(8,128)} %get-tuple-element.14), channel_id=1, source_target_pairs={{0,8},{4,12},{8,0},{12,4},{16,24},{20,28},{24,16},{28,20},{1,9},{5... | collective-permute-start | bytes 786440 | tf_op jit(solution)/shard_map/ppermute | solution.py:28
  453.4 32.6 %collective-permute-start.2 = (f32[1,32,16,128]{3,2,1,0:T(8,128)}, f32[1,32,16,128]{3,2,1,0:T(8,128)S(1)}, u32[]{:S(2)}, u32[]{:S(2)}) collective-permute-start(f32[1,32,16,128]{3,2,1,0:T(8,128)} %get-tuple-element.13), channel_id=1, source_target_pairs={{0,12},{4,8},{8,4},{12,0},{16,28},{20,24},{24,20},{28,16},{1,13},{... | collective-permute-start | bytes 786440 | tf_op jit(solution)/shard_map/ppermute | solution.py:28
  454.8 58.5 %collective-permute-start.3 = (f32[1,32,16,128]{3,2,1,0:T(8,128)S(1)}, f32[1,32,16,128]{3,2,1,0:T(8,128)S(1)}, u32[]{:S(2)}, u32[]{:S(2)}) collective-permute-start(f32[1,32,16,128]{3,2,1,0:T(8,128)S(1)} %get-tuple-element.12), channel_id=1, source_target_pairs={{0,16},{4,20},{8,24},{12,28},{16,0},{20,4},{24,8},{28,12},{1,17},{... | collective-permute-start | bytes 786440 | tf_op jit(solution)/shard_map/ppermute | solution.py:28
  457.2 61.7 %collective-permute-start.4 = (f32[1,32,16,128]{3,2,1,0:T(8,128)S(1)}, f32[1,32,16,128]{3,2,1,0:T(8,128)S(1)}, u32[]{:S(2)}, u32[]{:S(2)}) collective-permute-start(f32[1,32,16,128]{3,2,1,0:T(8,128)S(1)} %get-tuple-element.11), channel_id=1, source_target_pairs={{0,20},{4,16},{8,28},{12,24},{16,4},{20,0},{24,12},{28,8},{1,21},{... | collective-permute-start | bytes 786440 | tf_op jit(solution)/shard_map/ppermute | solution.py:28
  457.5 69.6 %collective-permute-start.5 = (f32[1,32,16,128]{3,2,1,0:T(8,128)S(1)}, f32[1,32,16,128]{3,2,1,0:T(8,128)S(1)}, u32[]{:S(2)}, u32[]{:S(2)}) collective-permute-start(f32[1,32,16,128]{3,2,1,0:T(8,128)S(1)} %get-tuple-element.10), channel_id=1, source_target_pairs={{0,24},{4,28},{8,16},{12,20},{16,8},{20,12},{24,0},{28,4},{1,25},{... | collective-permute-start | bytes 786440 | tf_op jit(solution)/shard_map/ppermute | solution.py:28
  480.8 50.8 %collective-permute-start.6 = (f32[1,32,16,128]{3,2,1,0:T(8,128)S(1)}, f32[1,32,16,128]{3,2,1,0:T(8,128)S(1)}, u32[]{:S(2)}, u32[]{:S(2)}) collective-permute-start(f32[1,32,16,128]{3,2,1,0:T(8,128)S(1)} %get-tuple-element.9), channel_id=1, source_target_pairs={{0,28},{4,24},{8,20},{12,16},{16,12},{20,8},{24,4},{28,0},{1,29},{... | collective-permute-start | bytes 786440 | tf_op jit(solution)/shard_map/ppermute | solution.py:28
  531.6 1.3 copy-start.7
Sparse Core Ops, SparseCore 0:
  16.1 176.7 all-reduce.2
